TPU v7x, 32 devices: a whole 2x2x4 slice. The times are simulated.
32 devices in a mesh: clip: 2 (over y), rows: 8 (over z, x), tm: 2 (over core).
Axes of the slice: x: 2, y: 2, z: 4, core: 2. Of those that a mesh axis runs over, the one named last changes fastest.
Arguments:
- latent: bfloat16 [8, 8, 64, 192], P(('clip', 'tm'), 'rows'), parts along dimension 0, may hold values from -18 to 18
- gain_first: bfloat16 [192], replicated, may hold values from 0.099609375 to 1.8984375
- conv_first: bfloat16 [3, 3, 3, 192, 192], replicated, may hold values from -0.078125 to 0.078125
- gain_second: bfloat16 [192], replicated, may hold values from 0.099609375 to 1.8984375
- conv_second: bfloat16 [3, 3, 3, 192, 192], replicated, may hold values from -0.078125 to 0.078125
- conv_up: bfloat16 [3, 3, 96, 192], replicated, may hold values from -0.15625 to 0.15625
Outputs:
- decoded: bfloat16 [8, 16, 96, 128], P(('clip', 'tm'), 'rows'), parts along dimension 0
- peaks: float32 [6, 192], P('clip'), parts along dimension 0
There are 2 independent parts, one for each index of `clip`. A program takes and returns all parts, laid end to end along the dimension named above; an argument that names none is the same for every part. Nothing has to cross between parts.
All inputs are finite; a program needn't handle non-finite values.
Results may differ from a plain program's by a relative error of at most 0.0085.
Values may be sent and summed in bfloat16 or wider, within the bound.
No kernel may reach another device: no remote copies, remote signals or barrier semaphores. Data moves between devices by JAX's collectives and lax.ppermute only.
A program may use at most 64 MiB of HBM per device.

v0:
```python
import functools

import jax
import jax.numpy as jnp
from jax import lax
from jax.experimental import pallas as pl
from jax.experimental.pallas import tpu as pltpu
from jax.sharding import PartitionSpec as P


EPS = 1e-06
LANES = 128
VMEM = pl.BlockSpec(memory_space=pltpu.VMEM)
FLOPS = 3_000_000_000
STAGE_FLOPS = 10_000_000_000


def swap_cores(block):
    return lax.ppermute(block, "tm", [(0, 1), (1, 0)])


def near_rows(block, distance):
    rows = lax.axis_size("rows")
    route = []
    for row in range(rows):
        down, up = row + distance, row - distance
        route.append((2 * row, 2 * down if down < rows else 2 * row + 1))
        route.append((2 * row + 1, 2 * up + 1 if up >= 0 else 2 * row))
    return lax.ppermute(block, ("rows", "tm"), route)


def slot_valid(slot):
    side = 1 - 2 * lax.axis_index("tm")
    at = lax.axis_index("rows") + slot * side
    return jnp.where((at >= 0) & (at < lax.axis_size("rows")), 1.0, 0.0)


def normed(floats, half_gain, channels, valid):
    mean = jnp.sum(floats * floats, axis=-1, keepdims=True) * (1.0 / channels)
    half = floats * (lax.rsqrt(mean + EPS) * valid) * half_gain
    return half + half * jnp.tanh(half)


def packing(channels):
    whole = channels // LANES * LANES
    rest = channels - whole
    return whole, rest, LANES // rest


def packed_plane(packed, frames, frame, place, channels):
    _, rest, count = packing(channels)
    low = packed[frame].astype(jnp.float32)
    high = packed[frames + lax.div(frame, count)].astype(jnp.float32)
    if place:
        high = pltpu.roll(high, LANES - place * rest, 1)
    lane = lax.broadcasted_iota(jnp.int32, high.shape, 1)
    return jnp.concatenate([low, jnp.where(lane < rest, high, 0.0)], axis=1)


def widened(plane, lanes):
    pad = jnp.zeros((plane.shape[0], lanes - plane.shape[1]), plane.dtype)
    return jnp.concatenate([plane, pad], axis=1)


def store_taps(taps, at, plane):
    edge = jnp.zeros((1, plane.shape[1]), plane.dtype)
    moved = (
        jnp.concatenate([edge, plane[:-1]], axis=0),
        plane,
        jnp.concatenate([plane[1:], edge], axis=0),
    )
    for tap, values in enumerate(moved):
        taps[(*at, tap)] = values.astype(jnp.bfloat16)


def slot_weights(weights, time_tap, row_taps, depth):
    core = lax.axis_index("tm")
    pad = jnp.zeros((depth - weights.shape[3], weights.shape[4]), weights.dtype)
    blocks = []
    for row_tap in row_taps:
        source = 2 * core + row_tap * (1 - 2 * core)
        for col_tap in range(3):
            blocks += [weights[time_tap, source, col_tap], pad]
    return jnp.concatenate(blocks, axis=0)


def causal(row_taps, planes, weights, total, base=None):
    slots, frames, cols, channels = total.shape
    for time_tap in (2, 1, 0):
        skip = 2 - time_tap
        pieces = []
        for refs in planes:
            for col_tap in range(3):
                parts = [ref[0, 0 : frames - skip, col_tap] for ref in refs]
                part = parts[0] if slots == 1 else jnp.concatenate(parts, axis=0)
                pieces.append(part.reshape(-1, part.shape[-1]))
        product = jnp.dot(
            jnp.concatenate(pieces, axis=-1),
            slot_weights(weights, time_tap, row_taps, pieces[0].shape[-1]),
            preferred_element_type=jnp.float32,
        ).reshape(slots, frames - skip, cols, channels)
        if skip == 0:
            total[...] = product if base is None else base[...] + product
        else:
            total[:, skip:] += product


def peak_of(plane):
    return jnp.max(jnp.abs(plane), axis=0, keepdims=True)


def rounded(values):
    return values.astype(jnp.bfloat16).astype(jnp.float32)


def stage_kernel(latent, staged):
    staged[...] = latent[...]


def join_kernel(mine, other, packed):
    frames, _, _, channels = mine.shape
    whole, _, count = packing(channels)
    clip_frames = 2 * frames
    first_core = lax.axis_index("tm") == 0
    planes = []
    for frame in range(clip_frames):
        near, far = (mine, other) if frame < frames else (other, mine)
        planes.append(jnp.where(first_core, near[frame % frames, 0], far[frame % frames, 0]))
    for frame, plane in enumerate(planes):
        packed[frame] = plane[:, :whole]
    for at in range(clip_frames // count):
        parts = [plane[:, whole:] for plane in planes[at * count : (at + 1) * count]]
        packed[clip_frames + at] = jnp.concatenate(parts, axis=1)


def own_kernel(own, gain_a, gain_b, weights, part_1, part_0, peak, half_a, half_b, taps):
    lanes = taps.shape[-1]
    channels = gain_a.shape[0]
    for gain, out in ((gain_a, half_a), (gain_b, half_b)):
        out[...] = widened(gain[...].reshape(1, -1).astype(jnp.float32) * 0.5, lanes)
    peak[...] = store_first(own, half_a, channels, 1.0, taps)
    causal((2,), ([taps],), weights, part_1)
    causal((1,), ([taps],), weights, part_0)


def store_first(packed, half_gain, channels, valid, taps):
    frames, lanes = taps.shape[1], taps.shape[-1]
    count = packing(channels)[2]
    top = jnp.zeros((1, lanes), jnp.float32)
    for frame in range(frames):
        plane = packed_plane(packed, frames, frame, frame % count, channels)
        first = normed(plane, half_gain[...], channels, valid)
        store_taps(taps, (0, frame), first)
        top = jnp.maximum(top, peak_of(first))
    return top


def store_second(total, half_gain, valid, taps, plain=None):
    frames, lanes = taps.shape[1], taps.shape[-1]
    top = jnp.zeros((1, lanes), jnp.float32)
    for frame in range(frames):
        hidden = widened(rounded(total[0, frame]), lanes)
        value = normed(hidden, half_gain[...], total.shape[-1], valid)
        store_taps(taps, (0, frame), value)
        if plain is not None:
            plain[frame] = value.astype(jnp.bfloat16)
        top = jnp.maximum(top, peak_of(value))
    return top


def near_kernel(
    near_1, near_2, part_1, half_a, half_b, weights, peak_in,
    near_taps, second_taps, second, part_2, peaks, outer_taps, total,
):
    channels = total.shape[-1]
    store_first(near_2, half_a, channels, slot_valid(-2), outer_taps)
    top = store_first(near_1, half_a, channels, slot_valid(-1), near_taps)
    peaks[0:1] = jnp.maximum(peak_in[...], top)
    causal((0, 1), ([outer_taps], [near_taps]), weights, total, part_1)
    causal((1, 2), ([outer_taps], [near_taps]), weights, part_2)
    peaks[1:2] = store_second(total, half_b, slot_valid(-1), second_taps, second)


def middle_kernel(
    far_1, near_3, near_taps, part_0, part_2, half_a, half_b, weights, peaks_in,
    taps_0, taps_2, second, peaks, far_taps, third_taps, total_0, total_2,
):
    channels = total_0.shape[-1]
    top = store_first(far_1, half_a, channels, slot_valid(1), far_taps)
    peaks[0:1] = jnp.maximum(peaks_in[0:1], top)
    store_first(near_3, half_a, channels, slot_valid(-3), third_taps)
    causal((0,), ([third_taps],), weights, total_2, part_2)
    causal((0, 2), ([near_taps], [far_taps]), weights, total_0, part_0)
    store_second(total_2, half_b, slot_valid(-2), taps_2, second)
    top = store_second(total_0, half_b, 1.0, taps_0)
    peaks[1:2] = jnp.maximum(peaks_in[1:2], top)


def merge(latents, slots, total, merged, top):
    out_frames = merged.shape[1]
    frames, _, channels = total.shape[1:]
    count = packing(channels)[2]
    core = lax.axis_index("tm")
    for place in range(frames):
        frame = lax.rem(core * out_frames + place, frames)
        for at, (latent, slot) in enumerate(zip(latents, slots)):
            plane = packed_plane(latent, frames, frame, place % count, channels)[:, :channels]
            value = (plane + total[at, frame]) * slot_valid(slot)
            top = jnp.maximum(top, peak_of(value))
            if place < out_frames:
                merged[at, place] = value.astype(jnp.bfloat16)
    return top


def inner_kernel(
    near_1, own, taps_2, taps_1, taps_0, second_far, weights, peaks_in,
    far_taps, merged, peaks, total,
):
    frames, _, channels = total.shape[1:]
    top = peaks_in[1:2]
    for frame in range(frames):
        value = second_far[frame].astype(jnp.float32)
        store_taps(far_taps, (0, frame), value)
        top = jnp.maximum(top, peak_of(value))
    peaks[0:1] = rounded(peaks_in[0:1])[:, :channels]
    peaks[1:2] = rounded(top)[:, :channels]
    causal((0, 1, 2), ([taps_2, taps_1], [taps_1, taps_0], [taps_0, far_taps]), weights, total)
    zero = jnp.zeros((1, channels), jnp.float32)
    peaks[2:3] = merge((near_1, own), (-1, 0), total, merged, zero)


def far_kernel(
    far_1, taps_0, far_taps, second_far, weights, peaks_in, merged, peaks, outer_taps, total
):
    for frame in range(total.shape[1]):
        store_taps(outer_taps, (0, frame), second_far[frame].astype(jnp.float32))
    causal((0, 1, 2), ([taps_0], [far_taps], [outer_taps]), weights, total)
    peaks[0:2] = peaks_in[0:2]
    peaks[2:3] = rounded(merge((far_1,), (1,), total, merged, peaks_in[2:3]))


def up_kernel(inner, outer, conv_up, decoded):
    frames, cols, _ = inner.shape[1:]
    first_core = lax.axis_index("tm") == 0
    out_channels = conv_up.shape[2]
    wide_cols = 2 * cols
    spread = jnp.where(
        lax.broadcasted_iota(jnp.int32, (wide_cols, cols), 0) // 2
        == lax.broadcasted_iota(jnp.int32, (wide_cols, cols), 1),
        1.0,
        0.0,
    ).astype(jnp.bfloat16)
    col = lax.broadcasted_iota(jnp.int32, (out_channels, wide_cols), 1)
    contract = (((1,), (1,)), ((), ()))
    sources = ((0, 1, 1), (1, 1, 2))
    for frame in range(frames):
        near, far = inner[0, frame], outer[0, frame]
        merged = (
            jnp.where(first_core, near, far),
            inner[1, frame],
            jnp.where(first_core, far, near),
        )
        wide = [
            jnp.dot(spread, row, preferred_element_type=jnp.float32).astype(jnp.bfloat16)
            for row in merged
        ]
        for half in range(2):
            sums = []
            for col_tap in range(3):
                total = None
                for row_tap in range(3):
                    term = lax.dot_general(
                        conv_up[row_tap, col_tap],
                        wide[sources[half][row_tap]],
                        contract,
                        preferred_element_type=jnp.float32,
                    )
                    total = term if total is None else total + term
                sums.append(total)
            left = jnp.where(col == 0, 0.0, pltpu.roll(sums[0], 1, 1))
            right = jnp.where(col == wide_cols - 1, 0.0, pltpu.roll(sums[2], wide_cols - 1, 1))
            decoded[frame, half] = (left + sums[1] + right).astype(jnp.bfloat16)


def peak_rounds(rows):
    bits = [1 << bit for bit in range(1, rows.bit_length() - 1)]
    rounds = []
    while bits:
        now, bits = bits[:2], bits[2:]
        rounds.append(now if len(now) == 1 else [now[0], now[1], now[0] | now[1]])
    return rounds


def group_peaks(peaks):
    rows = lax.axis_size("rows")
    for flips in peak_rounds(rows):
        arrived = []
        for flip in flips:
            arrived.append(lax.ppermute(peaks, "rows", [(r, r ^ flip) for r in range(rows)]))
        peaks = functools.reduce(jnp.maximum, arrived, peaks)
    return peaks


def per_device(latent, gain_first, conv_first, gain_second, conv_second, conv_up):
    frames, _, cols, channels = latent.shape
    clip_frames = lax.axis_size("tm") * frames
    lanes = -(-channels // LANES) * LANES
    bf16, f32 = jnp.bfloat16, jnp.float32
    taps_shape = (clip_frames, 3, cols, lanes)
    peaks_shape = jax.ShapeDtypeStruct((3, channels), f32)
    wide_peaks = jax.ShapeDtypeStruct((2, lanes), f32)
    row_shape = jax.ShapeDtypeStruct((1, lanes), f32)
    packed = clip_frames // packing(channels)[2] + clip_frames

    def call(kernel, outs, scratch, flops, *operands):
        return pl.pallas_call(
            kernel,
            out_shape=outs,
            in_specs=[VMEM] * len(operands),
            out_specs=jax.tree.map(lambda _: VMEM, outs),
            scratch_shapes=scratch,
            compiler_params=pltpu.CompilerParams(vmem_limit_bytes=16 << 20),
            cost_estimate=pl.CostEstimate(flops=flops, bytes_accessed=1 << 20, transcendentals=0),
        )(*operands)

    def totals(slots):
        return pltpu.VMEM((slots, clip_frames, cols, channels), f32)

    other = swap_cores(latent)
    mine = call(stage_kernel, jax.ShapeDtypeStruct(latent.shape, bf16), [], STAGE_FLOPS, latent)
    own = call(
        join_kernel, jax.ShapeDtypeStruct((packed, cols, LANES), bf16), [], FLOPS, mine, other
    )
    nears = []
    for distance in (1, 2, 3):
        nears.append(near_rows(own, distance))
    near_1, near_2, near_3 = nears
    taps_struct = jax.ShapeDtypeStruct((1, *taps_shape), bf16)
    taps_scratch = pltpu.VMEM((1, *taps_shape), bf16)
    plain = jax.ShapeDtypeStruct((clip_frames, cols, lanes), bf16)
    part = jax.ShapeDtypeStruct((1, clip_frames, cols, channels), f32)
    part_1, part_0, peak, half_a, half_b = call(
        own_kernel,
        (part, part, row_shape, row_shape, row_shape),
        [taps_scratch],
        FLOPS,
        own,
        gain_first,
        gain_second,
        conv_first,
    )
    near_1, part_1 = lax.optimization_barrier((near_1, part_1))
    far_1 = swap_cores(near_1)
    near_taps, taps_1, second_1, part_2, peaks = call(
        near_kernel,
        (taps_struct, taps_struct, plain, part, wide_peaks),
        [taps_scratch, totals(1)],
        FLOPS,
        near_1,
        near_2,
        part_1,
        half_a,
        half_b,
        conv_first,
        peak,
    )
    second_far_1 = swap_cores(second_1)
    taps_0, taps_2, second_2, peaks = call(
        middle_kernel,
        (taps_struct, taps_struct, plain, wide_peaks),
        [taps_scratch, taps_scratch, totals(1), totals(1)],
        FLOPS // 4,
        far_1,
        near_3,
        near_taps,
        part_0,
        part_2,
        half_a,
        half_b,
        conv_first,
        peaks,
    )
    second_far_2 = swap_cores(second_2)
    far_taps, merged, peaks = call(
        inner_kernel,
        (
            taps_struct,
            jax.ShapeDtypeStruct((2, frames, cols, channels), bf16),
            peaks_shape,
        ),
        [totals(2)],
        FLOPS,
        near_1,
        own,
        taps_2,
        taps_1,
        taps_0,
        second_far_1,
        conv_second,
        peaks,
    )
    merged_far, peaks = call(
        far_kernel,
        (jax.ShapeDtypeStruct((1, frames, cols, channels), bf16), peaks_shape),
        [taps_scratch, totals(1)],
        FLOPS,
        far_1,
        taps_0,
        far_taps,
        second_far_2,
        conv_second,
        peaks,
    )
    peaks = group_peaks(peaks)
    decoded = call(
        up_kernel,
        jax.ShapeDtypeStruct((frames, 2, conv_up.shape[2], 2 * cols), bf16),
        [],
        FLOPS,
        merged,
        merged_far,
        conv_up,
    )
    return decoded, peaks


def solution(mesh):
    return jax.shard_map(
        per_device,
        mesh=mesh,
        in_specs=(P(("clip", "tm"), "rows", None, None), P(), P(), P(), P(), P()),
        out_specs=(P(("clip", "tm"), "rows", None, None), P("clip", None)),
        check_vma=False,
    )
```

profile of v0, /device:TPU:0, one launch (start us, length us, event | category | flops | bytes accessed | tf_op | source)
XLA Modules:
  0.0 26.7 jit_solution(4087856851858134882)
XLA Ops:
  0.6 0.6 %collective-permute-start = (bf16[2,1,64,192]{3,2,1,0:T(8,128)(2,1)}, bf16[2,1,64,192]{3,2,1,0:T(8,128)(2,1)S(1)}, u32[]{:S(2)}, u32[]{:S(2)}) collective-permute-start(bf16[2,1,64,192]{3,2,1,0:T(8,128)(2,1)} %latent.1), channel_id=1, source_target_pairs={{0,1},{1,0},{2,3},{3,2},{4,5},{5,4},{6,7},{7,6},{8,9},{9,8},{10,11... | collective-permute-start | bytes 147464 | tf_op jit(solution)/shard_map/ppermute | solution.py:19
  1.2 0.8 %copy-done.3 = bf16[2,1,64,192]{3,2,1,0:T(8,128)(2,1)S(1)} copy-done((bf16[2,1,64,192]{3,2,1,0:T(8,128)(2,1)S(1)}, bf16[2,1,64,192]{3,2,1,0:T(8,128)(2,1)}, u32[]{:S(2)}) %copy-start.3) | copy-done | bytes 49176
  2.0 0.0 copy-start.4
  2.0 0.0 copy-start.5
  2.1 0.2 collective-permute-done.other
  2.3 0.1 shard_map.78.own
  2.4 2.9 %collective-permute-start.4 = (bf16[6,64,128]{2,1,0:T(8,128)(2,1)S(1)}, bf16[6,64,128]{2,1,0:T(8,128)(2,1)S(1)}, u32[]{:S(2)}, u32[]{:S(2)}) collective-permute-start(bf16[6,64,128]{2,1,0:T(8,128)(2,1)S(1)} %shard_map.78.own), channel_id=1, source_target_pairs={{0,4},{1,0},{2,6},{3,2},{4,8},{5,1},{6,10},{7,3},{8,12},{9,5},{10,... | collective-permute-start | bytes 294920 | tf_op jit(solution)/shard_map/ppermute | solution.py:29
  5.3 2.5 %collective-permute-start.3 = (bf16[6,64,128]{2,1,0:T(8,128)(2,1)S(1)}, bf16[6,64,128]{2,1,0:T(8,128)(2,1)S(1)}, u32[]{:S(2)}, u32[]{:S(2)}) collective-permute-start(bf16[6,64,128]{2,1,0:T(8,128)(2,1)S(1)} %shard_map.78.own), channel_id=1, source_target_pairs={{0,6},{1,0},{2,8},{3,2},{4,10},{5,4},{6,12},{7,1},{8,14},{9,3},{10... | collective-permute-start | bytes 294920 | tf_op jit(solution)/shard_map/ppermute | solution.py:29
  7.8 1.5 %collective-permute-start.1 = (bf16[6,64,128]{2,1,0:T(8,128)(2,1)S(1)}, bf16[6,64,128]{2,1,0:T(8,128)(2,1)S(1)}, u32[]{:S(2)}, u32[]{:S(2)}) collective-permute-start(bf16[6,64,128]{2,1,0:T(8,128)(2,1)S(1)} %shard_map.78.own), channel_id=1, source_target_pairs={{0,2},{1,0},{2,4},{3,1},{4,6},{5,3},{6,8},{7,5},{8,10},{9,7},{10,1... | collective-permute-start | bytes 294920 | tf_op jit(solution)/shard_map/ppermute | solution.py:29
  9.4 0.8 %shard_map.79 = (f32[1,4,64,192]{3,2,1,0:T(8,128)S(1)}, f32[1,4,64,192]{3,2,1,0:T(8,128)S(1)}, f32[1,256]{1,0:T(1,128)S(1)}, f32[1,256]{1,0:T(1,128)S(1)}, f32[1,256]{1,0:T(1,128)S(1)}) custom-call(bf16[6,64,128]{2,1,0:T(8,128)(2,1)S(1)} %shard_map.78.own, bf16[192]{0:T(256)(128)(2,1)S(1)} %copy-done.4, bf16[192]{0:T(256)(128)(2,1)S(1)} %copy-done.5, ...), custom_call_target="tpu_custom_call" | custom-call | flops 3000000000 | bytes 1048576 | tf_op jit(solution)/shard_map/pallas_call | solution.py:316
  10.2 1.4 %collective-permute-done.1.near_1 = bf16[6,64,128]{2,1,0:T(8,128)(2,1)S(1)} collective-permute-done((bf16[6,64,128]{2,1,0:T(8,128)(2,1)S(1)}, bf16[6,64,128]{2,1,0:T(8,128)(2,1)S(1)}, u32[]{:S(2)}, u32[]{:S(2)}) %collective-permute-start.1) | collective-permute-done | bytes 98336 | tf_op jit(solution)/shard_map/ppermute | solution.py:29
  11.6 1.4 %shard_map.80 = (bf16[1,4,3,64,256]{4,3,2,1,0:T(8,128)(2,1)S(1)}, bf16[1,4,3,64,256]{4,3,2,1,0:T(8,128)(2,1)S(1)}, bf16[4,64,256]{2,1,0:T(8,128)(2,1)S(1)}, f32[1,4,64,192]{3,2,1,0:T(8,128)S(1)}, f32[2,256]{1,0:T(2,128)S(1)}) custom-call(bf16[6,64,128]{2,1,0:T(8,128)(2,1)S(1)} %collective-permute-done.1.near_1, ...), custom_call_target="tpu_custom_call" | custom-call | flops 3000000000 | bytes 1048576 | tf_op jit(solution)/shard_map/pallas_call | solution.py:316
  13.0 0.6 %collective-permute-start.5 = (bf16[4,64,256]{2,1,0:T(8,128)(2,1)S(1)}, bf16[4,64,256]{2,1,0:T(8,128)(2,1)S(1)}, u32[]{:S(2)}, u32[]{:S(2)}) collective-permute-start(bf16[4,64,256]{2,1,0:T(8,128)(2,1)S(1)} %get-tuple-element.36), channel_id=1, source_target_pairs={{0,1},{1,0},{2,3},{3,2},{4,5},{5,4},{6,7},{7,6},{8,9},{9,8},{10,11... | collective-permute-start | bytes 393224 | tf_op jit(solution)/shard_map/ppermute | solution.py:19
  13.5 1.3 %shard_map.81 = (bf16[1,4,3,64,256]{4,3,2,1,0:T(8,128)(2,1)S(1)}, bf16[1,4,3,64,256]{4,3,2,1,0:T(8,128)(2,1)S(1)}, bf16[4,64,256]{2,1,0:T(8,128)(2,1)S(1)}, f32[2,256]{1,0:T(2,128)S(1)}) custom-call(bf16[6,64,128]{2,1,0:T(8,128)(2,1)S(1)} %collective-permute-done.2.far_1, bf16[6,64,128]{2,1,0:T(8,128)(2,1)S(1)} %collective-permute-done.3.near_3, ...), custom_call_target="tpu_custom_call" | custom-call | flops 750000000 | bytes 1048576 | tf_op jit(solution)/shard_map/pallas_call | solution.py:316
  14.8 0.1 collective-permute-start.6
  14.9 1.7 %shard_map.82 = (bf16[1,4,3,64,256]{4,3,2,1,0:T(8,128)(2,1)S(1)}, bf16[2,2,64,192]{3,2,1,0:T(8,128)(2,1)S(1)}, f32[3,192]{1,0:T(4,128)S(1)}) custom-call(bf16[6,64,128]{2,1,0:T(8,128)(2,1)S(1)} %collective-permute-done.1.near_1, bf16[6,64,128]{2,1,0:T(8,128)(2,1)S(1)} %shard_map.78.own, bf16[1,4,3,64,256]{4,3,2,1,0:T(8,128)(2,1)S(1)} %get-tuple-element.33.taps_2, ...), custom_call_target="tpu_custom_call" | custom-call | flops 3000000000 | bytes 1048576 | tf_op jit(solution)/shard_map/pallas_call | solution.py:316
  16.7 0.0 copy-start.2
  16.7 0.9 %shard_map.83 = (bf16[1,2,64,192]{3,2,1,0:T(8,128)(2,1)S(1)}, f32[3,192]{1,0:T(4,128)S(1)}) custom-call(bf16[6,64,128]{2,1,0:T(8,128)(2,1)S(1)} %collective-permute-done.2.far_1, bf16[1,4,3,64,256]{4,3,2,1,0:T(8,128)(2,1)S(1)} %get-tuple-element.35.taps_0, bf16[1,4,3,64,256]{4,3,2,1,0:T(8,128)(2,1)S(1)} %get-tuple-element.39.far_taps, ...), custom_call_target="tpu_custom_call" | custom-call | flops 3000000000 | bytes 1048576 | tf_op jit(solution)/shard_map/pallas_call | solution.py:316
  17.6 3.5 %collective-permute-start.9 = (f32[3,192]{1,0:T(4,128)S(1)}, f32[3,192]{1,0:T(4,128)S(1)}, u32[]{:S(2)}, u32[]{:S(2)}) collective-permute-start(f32[3,192]{1,0:T(4,128)S(1)} %get-tuple-element.43), channel_id=1, source_target_pairs={{0,12},{2,14},{4,8},{6,10},{8,4},{10,6},{12,0},{14,2},{1,13},{3,15... | collective-permute-start | bytes 6920 | tf_op jit(solution)/shard_map/ppermute | solution.py:299
  21.1 1.4 %collective-permute-start.8 = (f32[3,192]{1,0:T(4,128)S(1)}, f32[3,192]{1,0:T(4,128)S(1)}, u32[]{:S(2)}, u32[]{:S(2)}) collective-permute-start(f32[3,192]{1,0:T(4,128)S(1)} %get-tuple-element.43), channel_id=1, source_target_pairs={{0,8},{2,10},{4,12},{6,14},{8,0},{10,2},{12,4},{14,6},{1,9},{3,11}... | collective-permute-start | bytes 6920 | tf_op jit(solution)/shard_map/ppermute | solution.py:299
  22.5 1.9 %shard_map.84 = bf16[2,2,96,128]{3,2,1,0:T(8,128)(2,1)} custom-call(bf16[2,2,64,192]{3,2,1,0:T(8,128)(2,1)S(1)} %get-tuple-element.38.inner, bf16[1,2,64,192]{3,2,1,0:T(8,128)(2,1)S(1)} %get-tuple-element.42.outer, bf16[3,3,96,192]{3,2,1,0:T(8,128)(2,1)S(1)} %copy-done.2), custom_call_target="tpu_custom_call" | custom-call | flops 3000000000 | bytes 1048576 | tf_op jit(solution)/shard_map/pallas_call | solution.py:316
  24.4 1.2 %collective-permute-done.8 = f32[3,192]{1,0:T(4,128)S(1)} collective-permute-done((f32[3,192]{1,0:T(4,128)S(1)}, f32[3,192]{1,0:T(4,128)S(1)}, u32[]{:S(2)}, u32[]{:S(2)}) %collective-permute-start.8) | collective-permute-done | bytes 2336 | tf_op jit(solution)/shard_map/ppermute | solution.py:299
  25.6 0.5 %collective-permute-done.7 = f32[3,192]{1,0:T(4,128)S(1)} collective-permute-done((f32[3,192]{1,0:T(4,128)S(1)}, f32[3,192]{1,0:T(4,128)S(1)}, u32[]{:S(2)}, u32[]{:S(2)}) %collective-permute-start.7) | collective-permute-done | bytes 2336 | tf_op jit(solution)/shard_map/ppermute | solution.py:299
  26.1 0.6 %maximum_maximum_fusion = f32[3,192]{1,0:T(4,128)} fusion(f32[3,192]{1,0:T(4,128)S(1)} %collective-permute-done.9, f32[3,192]{1,0:T(4,128)S(1)} %collective-permute-done.8, f32[3,192]{1,0:T(4,128)S(1)} %get-tuple-element.43, f32[3,192]{1,0:T(4,128)S(1)} %collective-permute-done.7), kind=kLoop, calls=%fused_computation | loop fusion | flops 1728 | bytes 11520 | tf_op jit(solution)/shard_map/max | solution.py:300
  (17 shorter events, 0.0 us)
Async XLA Ops:
  0.6 1.7 %collective-permute-start = (bf16[2,1,64,192]{3,2,1,0:T(8,128)(2,1)}, bf16[2,1,64,192]{3,2,1,0:T(8,128)(2,1)S(1)}, u32[]{:S(2)}, u32[]{:S(2)}) collective-permute-start(bf16[2,1,64,192]{3,2,1,0:T(8,128)(2,1)} %latent.1), channel_id=1, source_target_pairs={{0,1},{1,0},{2,3},{3,2},{4,5},{5,4},{6,7},{7,6},{8,9},{9,8},{10,11... | collective-permute-start | bytes 147464 | tf_op jit(solution)/shard_map/ppermute | solution.py:19
  1.2 0.8 %copy-start.3 = (bf16[2,1,64,192]{3,2,1,0:T(8,128)(2,1)S(1)}, bf16[2,1,64,192]{3,2,1,0:T(8,128)(2,1)}, u32[]{:S(2)}) copy-start(bf16[2,1,64,192]{3,2,1,0:T(8,128)(2,1)} %latent.1) | copy-start | bytes 147460
  2.0 7.3 %copy-start = (bf16[3,3,3,192,192]{4,3,2,1,0:T(8,128)(2,1)S(1)}, bf16[3,3,3,192,192]{4,3,2,1,0:T(8,128)(2,1)}, u32[]{:S(2)}) copy-start(bf16[3,3,3,192,192]{4,3,2,1,0:T(8,128)(2,1)} %weights.7) | copy-start | bytes 5971972
  2.0 7.3 %copy-start.4 = (bf16[192]{0:T(256)(128)(2,1)S(1)}, bf16[192]{0:T(256)(128)(2,1)}, u32[]{:S(2)}) copy-start(bf16[192]{0:T(256)(128)(2,1)} %gain_a.1) | copy-start | bytes 1156
  2.0 7.3 %copy-start.5 = (bf16[192]{0:T(256)(128)(2,1)S(1)}, bf16[192]{0:T(256)(128)(2,1)}, u32[]{:S(2)}) copy-start(bf16[192]{0:T(256)(128)(2,1)} %gain_b.1) | copy-start | bytes 1156
  2.4 9.2 %collective-permute-start.4 = (bf16[6,64,128]{2,1,0:T(8,128)(2,1)S(1)}, bf16[6,64,128]{2,1,0:T(8,128)(2,1)S(1)}, u32[]{:S(2)}, u32[]{:S(2)}) collective-permute-start(bf16[6,64,128]{2,1,0:T(8,128)(2,1)S(1)} %shard_map.78.own), channel_id=1, source_target_pairs={{0,4},{1,0},{2,6},{3,2},{4,8},{5,1},{6,10},{7,3},{8,12},{9,5},{10,... | collective-permute-start | bytes 294920 | tf_op jit(solution)/shard_map/ppermute | solution.py:29
  5.3 8.2 %collective-permute-start.3 = (bf16[6,64,128]{2,1,0:T(8,128)(2,1)S(1)}, bf16[6,64,128]{2,1,0:T(8,128)(2,1)S(1)}, u32[]{:S(2)}, u32[]{:S(2)}) collective-permute-start(bf16[6,64,128]{2,1,0:T(8,128)(2,1)S(1)} %shard_map.78.own), channel_id=1, source_target_pairs={{0,6},{1,0},{2,8},{3,2},{4,10},{5,4},{6,12},{7,1},{8,14},{9,3},{10... | collective-permute-start | bytes 294920 | tf_op jit(solution)/shard_map/ppermute | solution.py:29
  7.8 3.8 %collective-permute-start.1 = (bf16[6,64,128]{2,1,0:T(8,128)(2,1)S(1)}, bf16[6,64,128]{2,1,0:T(8,128)(2,1)S(1)}, u32[]{:S(2)}, u32[]{:S(2)}) collective-permute-start(bf16[6,64,128]{2,1,0:T(8,128)(2,1)S(1)} %shard_map.78.own), channel_id=1, source_target_pairs={{0,2},{1,0},{2,4},{3,1},{4,6},{5,3},{6,8},{7,5},{8,10},{9,7},{10,1... | collective-permute-start | bytes 294920 | tf_op jit(solution)/shard_map/ppermute | solution.py:29
  11.6 2.0 %collective-permute-start.2 = (bf16[6,64,128]{2,1,0:T(8,128)(2,1)S(1)}, bf16[6,64,128]{2,1,0:T(8,128)(2,1)S(1)}, u32[]{:S(2)}, u32[]{:S(2)}) collective-permute-start(bf16[6,64,128]{2,1,0:T(8,128)(2,1)S(1)} %collective-permute-done.1.near_1), channel_id=1, source_target_pairs={{0,1},{1,0},{2,3},{3,2},{4,5},{5,4},{6,7},{7,6},{8,9},{9,8},{10,11... | collective-permute-start | bytes 294920 | tf_op jit(solution)/shard_map/ppermute | solution.py:19
  13.0 2.0 %copy-start.1 = (bf16[3,3,3,192,192]{4,3,2,1,0:T(8,128)(2,1)S(1)}, bf16[3,3,3,192,192]{4,3,2,1,0:T(8,128)(2,1)}, u32[]{:S(2)}) copy-start(bf16[3,3,3,192,192]{4,3,2,1,0:T(8,128)(2,1)} %weights.9) | copy-start | bytes 5971972
  13.0 2.0 %collective-permute-start.5 = (bf16[4,64,256]{2,1,0:T(8,128)(2,1)S(1)}, bf16[4,64,256]{2,1,0:T(8,128)(2,1)S(1)}, u32[]{:S(2)}, u32[]{:S(2)}) collective-permute-start(bf16[4,64,256]{2,1,0:T(8,128)(2,1)S(1)} %get-tuple-element.36), channel_id=1, source_target_pairs={{0,1},{1,0},{2,3},{3,2},{4,5},{5,4},{6,7},{7,6},{8,9},{9,8},{10,11... | collective-permute-start | bytes 393224 | tf_op jit(solution)/shard_map/ppermute | solution.py:19
  14.8 1.8 %collective-permute-start.6 = (bf16[4,64,256]{2,1,0:T(8,128)(2,1)S(1)}, bf16[4,64,256]{2,1,0:T(8,128)(2,1)S(1)}, u32[]{:S(2)}, u32[]{:S(2)}) collective-permute-start(bf16[4,64,256]{2,1,0:T(8,128)(2,1)S(1)} %get-tuple-element.40), channel_id=1, source_target_pairs={{0,1},{1,0},{2,3},{3,2},{4,5},{5,4},{6,7},{7,6},{8,9},{9,8},{10,11... | collective-permute-start | bytes 393224 | tf_op jit(solution)/shard_map/ppermute | solution.py:19
  16.7 5.8 %copy-start.2 = (bf16[3,3,96,192]{3,2,1,0:T(8,128)(2,1)S(1)}, bf16[3,3,96,192]{3,2,1,0:T(8,128)(2,1)}, u32[]{:S(2)}) copy-start(bf16[3,3,96,192]{3,2,1,0:T(8,128)(2,1)} %conv_up.1) | copy-start | bytes 995332
  17.6 6.8 %collective-permute-start.9 = (f32[3,192]{1,0:T(4,128)S(1)}, f32[3,192]{1,0:T(4,128)S(1)}, u32[]{:S(2)}, u32[]{:S(2)}) collective-permute-start(f32[3,192]{1,0:T(4,128)S(1)} %get-tuple-element.43), channel_id=1, source_target_pairs={{0,12},{2,14},{4,8},{6,10},{8,4},{10,6},{12,0},{14,2},{1,13},{3,15... | collective-permute-start | bytes 6920 | tf_op jit(solution)/shard_map/ppermute | solution.py:299
  21.1 4.5 %collective-permute-start.8 = (f32[3,192]{1,0:T(4,128)S(1)}, f32[3,192]{1,0:T(4,128)S(1)}, u32[]{:S(2)}, u32[]{:S(2)}) collective-permute-start(f32[3,192]{1,0:T(4,128)S(1)} %get-tuple-element.43), channel_id=1, source_target_pairs={{0,8},{2,10},{4,12},{6,14},{8,0},{10,2},{12,4},{14,6},{1,9},{3,11}... | collective-permute-start | bytes 6920 | tf_op jit(solution)/shard_map/ppermute | solution.py:299
  22.5 3.6 %collective-permute-start.7 = (f32[3,192]{1,0:T(4,128)S(1)}, f32[3,192]{1,0:T(4,128)S(1)}, u32[]{:S(2)}, u32[]{:S(2)}) collective-permute-start(f32[3,192]{1,0:T(4,128)S(1)} %get-tuple-element.43), channel_id=1, source_target_pairs={{0,4},{2,6},{4,0},{6,2},{8,12},{10,14},{12,8},{14,10},{1,5},{3,7},... | collective-permute-start | bytes 6920 | tf_op jit(solution)/shard_map/ppermute | solution.py:299
where the time goes:
time: 26.8 us; the launch traced here: 26.7 us
  starting transfers between devices  13.1 us (49%)
  Pallas kernels  8.16 us (30%)
  waiting for transfers between devices  3.31 us (12%)
  local copies, waits for them, and re-layouts  0.87 us (3%)
  between operations  0.71 us (3%)
  other arithmetic  0.6 us (2%)
    pallas_call x8, Pallas kernels, call(): pl.pallas_call(kernel, out_shape=outs, in_specs=[VMEM] * len(operands), o...  8.16 us
    ppermute x3, starting transfers between devices, near_rows(): return lax.ppermute(block, ('rows', 'tm'), route)  6.96 us
    ppermute x3, starting transfers between devices, group_peaks(): lax.ppermute(peaks, 'rows', [(r, r ^ flip) for r in range(rows)])  4.86 us
    ppermute x3, waiting for transfers between devices, group_peaks(): lax.ppermute(peaks, 'rows', [(r, r ^ flip) for r in range(rows)])  1.67 us
    ppermute x3, waiting for transfers between devices, near_rows(): return lax.ppermute(block, ('rows', 'tm'), route)  1.39 us
    ppermute x4, starting transfers between devices, swap_cores(): return lax.ppermute(block, 'tm', [(0, 1), (1, 0)])  1.23 us
    unnamed x12, local copies, waits for them, and re-layouts  0.87 us
    max x1, other arithmetic, group_peaks(): peaks = functools.reduce(jnp.maximum, arrived, peaks)  0.6 us
  transfers between devices with their start and end apart: 10, of which 4 were waited for; matrix products, arithmetic and copies ran while one was open for 0% of the time, Pallas kernels for 27%

commit v1 on v0

--- a/solution.py
+++ b/solution.py
@@ -10,6 +10,7 @@
 
 EPS = 1e-06
 LANES = 128
+PEAK_ROWS = 16
 VMEM = pl.BlockSpec(memory_space=pltpu.VMEM)
 FLOPS = 3_000_000_000
 STAGE_FLOPS = 10_000_000_000
@@ -183,7 +184,7 @@
 
 def middle_kernel(
     far_1, near_3, near_taps, part_0, part_2, half_a, half_b, weights, peaks_in,
-    taps_0, taps_2, second, peaks, far_taps, third_taps, total_0, total_2,
+    taps_0, taps_2, peaks, far_taps, third_taps, total_0, total_2,
 ):
     channels = total_0.shape[-1]
     top = store_first(far_1, half_a, channels, slot_valid(1), far_taps)
@@ -191,31 +192,36 @@
     store_first(near_3, half_a, channels, slot_valid(-3), third_taps)
     causal((0,), ([third_taps],), weights, total_2, part_2)
     causal((0, 2), ([near_taps], [far_taps]), weights, total_0, part_0)
-    store_second(total_2, half_b, slot_valid(-2), taps_2, second)
+    store_second(total_2, half_b, slot_valid(-2), taps_2)
     top = store_second(total_0, half_b, 1.0, taps_0)
     peaks[1:2] = jnp.maximum(peaks_in[1:2], top)
 
 
-def merge(latents, slots, total, merged, top):
-    out_frames = merged.shape[1]
+def merge(latent, slot, total, merged):
     frames, _, channels = total.shape[1:]
     count = packing(channels)[2]
-    core = lax.axis_index("tm")
-    for place in range(frames):
-        frame = lax.rem(core * out_frames + place, frames)
-        for at, (latent, slot) in enumerate(zip(latents, slots)):
-            plane = packed_plane(latent, frames, frame, place % count, channels)[:, :channels]
-            value = (plane + total[at, frame]) * slot_valid(slot)
-            top = jnp.maximum(top, peak_of(value))
-            if place < out_frames:
-                merged[at, place] = value.astype(jnp.bfloat16)
+    top = jnp.zeros((1, channels), jnp.float32)
+    for frame in range(frames):
+        plane = packed_plane(latent, frames, frame, frame % count, channels)[:, :channels]
+        value = (plane + total[0, frame]) * slot_valid(slot)
+        top = jnp.maximum(top, peak_of(value))
+        merged[frame] = value.astype(jnp.bfloat16)
     return top
 
 
-def inner_kernel(
-    near_1, own, taps_2, taps_1, taps_0, second_far, weights, peaks_in,
-    far_taps, merged, peaks, total,
-):
+def side_kernel(near_1, taps_2, taps_1, taps_0, weights, merged, sent, total):
+    frames, cols, _ = merged.shape
+    count = frames // 2
+    causal((0, 1, 2), ([taps_2], [taps_1], [taps_0]), weights, total)
+    top = merge(near_1, -1, total, merged)
+    other = 1 - lax.axis_index("tm")
+    for place in range(count):
+        sent[place * cols : (place + 1) * cols] = merged[other * count + place]
+    rest = sent.shape[0] - count * cols
+    sent[count * cols :] = jnp.broadcast_to(top, (rest, top.shape[1])).astype(jnp.bfloat16)
+
+
+def inner_kernel(own, taps_1, taps_0, second_far, weights, peaks_in, merged, peaks, far_taps, total):
     frames, _, channels = total.shape[1:]
     top = peaks_in[1:2]
     for frame in range(frames):
@@ -224,26 +230,14 @@
         top = jnp.maximum(top, peak_of(value))
     peaks[0:1] = rounded(peaks_in[0:1])[:, :channels]
     peaks[1:2] = rounded(top)[:, :channels]
-    causal((0, 1, 2), ([taps_2, taps_1], [taps_1, taps_0], [taps_0, far_taps]), weights, total)
-    zero = jnp.zeros((1, channels), jnp.float32)
-    peaks[2:3] = merge((near_1, own), (-1, 0), total, merged, zero)
-
-
-def far_kernel(
-    far_1, taps_0, far_taps, second_far, weights, peaks_in, merged, peaks, outer_taps, total
-):
-    for frame in range(total.shape[1]):
-        store_taps(outer_taps, (0, frame), second_far[frame].astype(jnp.float32))
-    causal((0, 1, 2), ([taps_0], [far_taps], [outer_taps]), weights, total)
-    peaks[0:2] = peaks_in[0:2]
-    peaks[2:3] = rounded(merge((far_1,), (1,), total, merged, peaks_in[2:3]))
-
-
-def up_kernel(inner, outer, conv_up, decoded):
-    frames, cols, _ = inner.shape[1:]
-    first_core = lax.axis_index("tm") == 0
-    out_channels = conv_up.shape[2]
-    wide_cols = 2 * cols
+    causal((0, 1, 2), ([taps_1], [taps_0], [far_taps]), weights, total)
+    peaks[2:3] = rounded(merge(own, 0, total, merged))
+
+
+def up_kernel(near_merged, own_merged, far_merged, conv_up, decoded):
+    frames, _, out_channels, wide_cols = decoded.shape
+    cols = own_merged.shape[1]
+    core = lax.axis_index("tm")
     spread = jnp.where(
         lax.broadcasted_iota(jnp.int32, (wide_cols, cols), 0) // 2
         == lax.broadcasted_iota(jnp.int32, (wide_cols, cols), 1),
@@ -251,35 +245,34 @@
         0.0,
     ).astype(jnp.bfloat16)
     col = lax.broadcasted_iota(jnp.int32, (out_channels, wide_cols), 1)
-    contract = (((1,), (1,)), ((), ()))
-    sources = ((0, 1, 1), (1, 1, 2))
-    for frame in range(frames):
-        near, far = inner[0, frame], outer[0, frame]
-        merged = (
-            jnp.where(first_core, near, far),
-            inner[1, frame],
-            jnp.where(first_core, far, near),
+
+    def products(row, row_taps):
+        wide = jnp.dot(spread, row, preferred_element_type=jnp.float32).astype(jnp.bfloat16)
+        taps = conv_up[row_taps[0] : row_taps[-1] + 1]
+        result = lax.dot_general(
+            taps.reshape(-1, taps.shape[-1]),
+            wide,
+            (((1,), (1,)), ((), ())),
+            preferred_element_type=jnp.float32,
         )
-        wide = [
-            jnp.dot(spread, row, preferred_element_type=jnp.float32).astype(jnp.bfloat16)
-            for row in merged
-        ]
+        return result.reshape(len(row_taps), 3, out_channels, wide_cols)
+
+    for place in range(frames):
+        frame = core * frames + place
+        near, far = near_merged[frame], far_merged[place * cols : (place + 1) * cols]
+        above = products(jnp.where(core == 0, near, far), (0,))
+        below = products(jnp.where(core == 0, far, near), (2,))
+        middle = products(own_merged[frame], (0, 1, 2))
         for half in range(2):
             sums = []
-            for col_tap in range(3):
-                total = None
-                for row_tap in range(3):
-                    term = lax.dot_general(
-                        conv_up[row_tap, col_tap],
-                        wide[sources[half][row_tap]],
-                        contract,
-                        preferred_element_type=jnp.float32,
-                    )
-                    total = term if total is None else total + term
-                sums.append(total)
+            for tap in range(3):
+                if half == 0:
+                    sums.append(above[0, tap] + middle[1, tap] + middle[2, tap])
+                else:
+                    sums.append(middle[0, tap] + middle[1, tap] + below[0, tap])
             left = jnp.where(col == 0, 0.0, pltpu.roll(sums[0], 1, 1))
             right = jnp.where(col == wide_cols - 1, 0.0, pltpu.roll(sums[2], wide_cols - 1, 1))
-            decoded[frame, half] = (left + sums[1] + right).astype(jnp.bfloat16)
+            decoded[place, half] = (left + sums[1] + right).astype(jnp.bfloat16)
 
 
 def peak_rounds(rows):
@@ -365,9 +358,9 @@
         peak,
     )
     second_far_1 = swap_cores(second_1)
-    taps_0, taps_2, second_2, peaks = call(
+    taps_0, taps_2, peaks = call(
         middle_kernel,
-        (taps_struct, taps_struct, plain, wide_peaks),
+        (taps_struct, taps_struct, wide_peaks),
         [taps_scratch, taps_scratch, totals(1), totals(1)],
         FLOPS // 4,
         far_1,
@@ -380,44 +373,44 @@
         conv_first,
         peaks,
     )
-    second_far_2 = swap_cores(second_2)
-    far_taps, merged, peaks = call(
-        inner_kernel,
+    merged_struct = jax.ShapeDtypeStruct((clip_frames, cols, channels), bf16)
+    merged_near, sent = call(
+        side_kernel,
         (
-            taps_struct,
-            jax.ShapeDtypeStruct((2, frames, cols, channels), bf16),
-            peaks_shape,
+            merged_struct,
+            jax.ShapeDtypeStruct((frames * cols + PEAK_ROWS, channels), bf16),
         ),
-        [totals(2)],
+        [totals(1)],
         FLOPS,
         near_1,
+        taps_2,
+        taps_1,
+        taps_0,
+        conv_second,
+    )
+    merged_far = swap_cores(sent)
+    merged_own, peaks = call(
+        inner_kernel,
+        (merged_struct, peaks_shape),
+        [taps_scratch, totals(1)],
+        FLOPS,
         own,
-        taps_2,
         taps_1,
         taps_0,
         second_far_1,
         conv_second,
         peaks,
     )
-    merged_far, peaks = call(
-        far_kernel,
-        (jax.ShapeDtypeStruct((1, frames, cols, channels), bf16), peaks_shape),
-        [taps_scratch, totals(1)],
-        FLOPS,
-        far_1,
-        taps_0,
-        far_taps,
-        second_far_2,
-        conv_second,
-        peaks,
-    )
+    sides = jnp.maximum(sent[frames * cols], merged_far[frames * cols]).astype(f32)
+    peaks = jnp.maximum(peaks, jnp.stack([jnp.zeros_like(sides)] * 2 + [sides]))
     peaks = group_peaks(peaks)
     decoded = call(
         up_kernel,
         jax.ShapeDtypeStruct((frames, 2, conv_up.shape[2], 2 * cols), bf16),
         [],
         FLOPS,
-        merged,
+        merged_near,
+        merged_own,
         merged_far,
         conv_up,
     )

time: 26.8 us -> 27.3 us (1.019)
  starting transfers between devices: 13.1 us -> 14.3 us
  Pallas kernels: 8.16 us -> 7.28 us
    ppermute x3, starting transfers between devices: 4.86 us -> 5.77 us  [group_peaks(): lax.ppermute(peaks, 'rows', [(r, r ^ flip) for r in range(rows)])]
    pallas_call x8, Pallas kernels: 8.16 us -> 7.28 us  [call(): pl.pallas_call(kernel, out_shape=outs, in_specs=[VMEM] * len(operands), o...]
    ppermute x4, starting transfers between devices: 1.23 us -> 1.54 us  [swap_cores(): return lax.ppermute(block, 'tm', [(0, 1), (1, 0)])]
where the time goes in v1:
time: 27.3 us; the launch traced here: 27.1 us
  starting transfers between devices  14.3 us (52%)
  Pallas kernels  7.28 us (27%)
  waiting for transfers between devices  3.36 us (12%)
  local copies, waits for them, and re-layouts  0.87 us (3%)
  between operations  0.72 us (3%)
  other arithmetic  0.62 us (2%)
    pallas_call x8, Pallas kernels, call(): pl.pallas_call(kernel, out_shape=outs, in_specs=[VMEM] * len(operands), o...  7.28 us
    ppermute x3, starting transfers between devices, near_rows(): return lax.ppermute(block, ('rows', 'tm'), route)  6.96 us
    ppermute x3, starting transfers between devices, group_peaks(): lax.ppermute(peaks, 'rows', [(r, r ^ flip) for r in range(rows)])  5.77 us
    ppermute x3, waiting for transfers between devices, group_peaks(): lax.ppermute(peaks, 'rows', [(r, r ^ flip) for r in range(rows)])  1.72 us
    ppermute x4, starting transfers between devices, swap_cores(): return lax.ppermute(block, 'tm', [(0, 1), (1, 0)])  1.54 us
    ppermute x3, waiting for transfers between devices, near_rows(): return lax.ppermute(block, ('rows', 'tm'), route)  1.39 us
    unnamed x12, local copies, waits for them, and re-layouts  0.87 us
    max x1, other arithmetic, group_peaks(): peaks = functools.reduce(jnp.maximum, arrived, peaks)  0.6 us
  transfers between devices with their start and end apart: 10, of which 4 were waited for; matrix products, arithmetic and copies ran while one was open for 0% of the time, Pallas kernels for 27%

profile of v1, /device:TPU:0, one launch (start us, length us, event | category | flops | bytes accessed | tf_op | source)
XLA Modules:
  0.0 27.1 jit_solution(16769228568954451947)
XLA Ops:
  0.6 0.6 %collective-permute-start = (bf16[2,1,64,192]{3,2,1,0:T(8,128)(2,1)}, bf16[2,1,64,192]{3,2,1,0:T(8,128)(2,1)S(1)}, u32[]{:S(2)}, u32[]{:S(2)}) collective-permute-start(bf16[2,1,64,192]{3,2,1,0:T(8,128)(2,1)} %latent.1), channel_id=1, source_target_pairs={{0,1},{1,0},{2,3},{3,2},{4,5},{5,4},{6,7},{7,6},{8,9},{9,8},{10,11... | collective-permute-start | bytes 147464 | tf_op jit(solution)/shard_map/ppermute | solution.py:20
  1.2 0.8 %copy-done.3 = bf16[2,1,64,192]{3,2,1,0:T(8,128)(2,1)S(1)} copy-done((bf16[2,1,64,192]{3,2,1,0:T(8,128)(2,1)S(1)}, bf16[2,1,64,192]{3,2,1,0:T(8,128)(2,1)}, u32[]{:S(2)}) %copy-start.3) | copy-done | bytes 49176
  2.0 0.0 copy-start.4
  2.0 0.0 copy-start.5
  2.1 0.2 collective-permute-done.other
  2.3 0.1 shard_map.78.own
  2.4 2.9 %collective-permute-start.4 = (bf16[6,64,128]{2,1,0:T(8,128)(2,1)S(1)}, bf16[6,64,128]{2,1,0:T(8,128)(2,1)S(1)}, u32[]{:S(2)}, u32[]{:S(2)}) collective-permute-start(bf16[6,64,128]{2,1,0:T(8,128)(2,1)S(1)} %shard_map.78.own), channel_id=1, source_target_pairs={{0,4},{1,0},{2,6},{3,2},{4,8},{5,1},{6,10},{7,3},{8,12},{9,5},{10,... | collective-permute-start | bytes 294920 | tf_op jit(solution)/shard_map/ppermute | solution.py:30
  5.3 2.5 %collective-permute-start.3 = (bf16[6,64,128]{2,1,0:T(8,128)(2,1)S(1)}, bf16[6,64,128]{2,1,0:T(8,128)(2,1)S(1)}, u32[]{:S(2)}, u32[]{:S(2)}) collective-permute-start(bf16[6,64,128]{2,1,0:T(8,128)(2,1)S(1)} %shard_map.78.own), channel_id=1, source_target_pairs={{0,6},{1,0},{2,8},{3,2},{4,10},{5,4},{6,12},{7,1},{8,14},{9,3},{10... | collective-permute-start | bytes 294920 | tf_op jit(solution)/shard_map/ppermute | solution.py:30
  7.8 1.5 %collective-permute-start.1 = (bf16[6,64,128]{2,1,0:T(8,128)(2,1)S(1)}, bf16[6,64,128]{2,1,0:T(8,128)(2,1)S(1)}, u32[]{:S(2)}, u32[]{:S(2)}) collective-permute-start(bf16[6,64,128]{2,1,0:T(8,128)(2,1)S(1)} %shard_map.78.own), channel_id=1, source_target_pairs={{0,2},{1,0},{2,4},{3,1},{4,6},{5,3},{6,8},{7,5},{8,10},{9,7},{10,1... | collective-permute-start | bytes 294920 | tf_op jit(solution)/shard_map/ppermute | solution.py:30
  9.4 0.8 %shard_map.79 = (f32[1,4,64,192]{3,2,1,0:T(8,128)S(1)}, f32[1,4,64,192]{3,2,1,0:T(8,128)S(1)}, f32[1,256]{1,0:T(1,128)S(1)}, f32[1,256]{1,0:T(1,128)S(1)}, f32[1,256]{1,0:T(1,128)S(1)}) custom-call(bf16[6,64,128]{2,1,0:T(8,128)(2,1)S(1)} %shard_map.78.own, bf16[192]{0:T(256)(128)(2,1)S(1)} %copy-done.4, bf16[192]{0:T(256)(128)(2,1)S(1)} %copy-done.5, ...), custom_call_target="tpu_custom_call" | custom-call | flops 3000000000 | bytes 1048576 | tf_op jit(solution)/shard_map/pallas_call | solution.py:309
  10.2 1.4 %collective-permute-done.1.near_1 = bf16[6,64,128]{2,1,0:T(8,128)(2,1)S(1)} collective-permute-done((bf16[6,64,128]{2,1,0:T(8,128)(2,1)S(1)}, bf16[6,64,128]{2,1,0:T(8,128)(2,1)S(1)}, u32[]{:S(2)}, u32[]{:S(2)}) %collective-permute-start.1) | collective-permute-done | bytes 98336 | tf_op jit(solution)/shard_map/ppermute | solution.py:30
  11.6 1.4 %shard_map.80 = (bf16[1,4,3,64,256]{4,3,2,1,0:T(8,128)(2,1)S(1)}, bf16[1,4,3,64,256]{4,3,2,1,0:T(8,128)(2,1)S(1)}, bf16[4,64,256]{2,1,0:T(8,128)(2,1)S(1)}, f32[1,4,64,192]{3,2,1,0:T(8,128)S(1)}, f32[2,256]{1,0:T(2,128)S(1)}) custom-call(bf16[6,64,128]{2,1,0:T(8,128)(2,1)S(1)} %collective-permute-done.1.near_1, ...), custom_call_target="tpu_custom_call" | custom-call | flops 3000000000 | bytes 1048576 | tf_op jit(solution)/shard_map/pallas_call | solution.py:309
  13.0 0.0 copy-start.1
  13.0 0.6 %collective-permute-start.5 = (bf16[4,64,256]{2,1,0:T(8,128)(2,1)S(1)}, bf16[4,64,256]{2,1,0:T(8,128)(2,1)S(1)}, u32[]{:S(2)}, u32[]{:S(2)}) collective-permute-start(bf16[4,64,256]{2,1,0:T(8,128)(2,1)S(1)} %get-tuple-element.35), channel_id=1, source_target_pairs={{0,1},{1,0},{2,3},{3,2},{4,5},{5,4},{6,7},{7,6},{8,9},{9,8},{10,11... | collective-permute-start | bytes 393224 | tf_op jit(solution)/shard_map/ppermute | solution.py:20
  13.5 1.3 %shard_map.81 = (bf16[1,4,3,64,256]{4,3,2,1,0:T(8,128)(2,1)S(1)}, bf16[1,4,3,64,256]{4,3,2,1,0:T(8,128)(2,1)S(1)}, f32[2,256]{1,0:T(2,128)S(1)}) custom-call(bf16[6,64,128]{2,1,0:T(8,128)(2,1)S(1)} %collective-permute-done.2.far_1, bf16[6,64,128]{2,1,0:T(8,128)(2,1)S(1)} %collective-permute-done.3.near_3, ...), custom_call_target="tpu_custom_call" | custom-call | flops 750000000 | bytes 1048576 | tf_op jit(solution)/shard_map/pallas_call | solution.py:309
  14.8 0.9 %shard_map.82 = (bf16[4,64,192]{2,1,0:T(8,128)(2,1)S(1)}, bf16[144,192]{1,0:T(8,128)(2,1)S(1)}) custom-call(bf16[6,64,128]{2,1,0:T(8,128)(2,1)S(1)} %collective-permute-done.1.near_1, bf16[1,4,3,64,256]{4,3,2,1,0:T(8,128)(2,1)S(1)} %get-tuple-element.31.taps_2, bf16[1,4,3,64,256]{4,3,2,1,0:T(8,128)(2,1)S(1)} %get-tuple-element.32.taps_1, ...), custom_call_target="tpu_custom_call" | custom-call | flops 3000000000 | bytes 1048576 | tf_op jit(solution)/shard_map/pallas_call | solution.py:309
  15.8 0.4 %collective-permute-start.6 = (bf16[144,192]{1,0:T(8,128)(2,1)S(1)}, bf16[144,192]{1,0:T(8,128)(2,1)S(1)}, u32[]{:S(2)}, u32[]{:S(2)}) collective-permute-start(bf16[144,192]{1,0:T(8,128)(2,1)S(1)} %get-tuple-element.38), channel_id=1, source_target_pairs={{0,1},{1,0},{2,3},{3,2},{4,5},{5,4},{6,7},{7,6},{8,9},{9,8},{10,11... | collective-permute-start | bytes 165896 | tf_op jit(solution)/shard_map/ppermute | solution.py:20
  16.2 0.9 %shard_map.83 = (bf16[4,64,192]{2,1,0:T(8,128)(2,1)S(1)}, f32[3,192]{1,0:T(4,128)S(1)}) custom-call(bf16[6,64,128]{2,1,0:T(8,128)(2,1)S(1)} %shard_map.78.own, bf16[1,4,3,64,256]{4,3,2,1,0:T(8,128)(2,1)S(1)} %get-tuple-element.32.taps_1, bf16[1,4,3,64,256]{4,3,2,1,0:T(8,128)(2,1)S(1)} %get-tuple-element.33.taps_0, ...), custom_call_target="tpu_custom_call" | custom-call | flops 3000000000 | bytes 1048576 | tf_op jit(solution)/shard_map/pallas_call | solution.py:309
  17.1 3.9 %collective-permute-start.8 = (f32[3,192]{1,0:T(4,128)S(1)}, f32[3,192]{1,0:T(4,128)S(1)}, u32[]{:S(2)}, u32[]{:S(2)}) collective-permute-start(f32[3,192]{1,0:T(4,128)S(1)} %convert_maximum_fusion), channel_id=1, source_target_pairs={{0,8},{2,10},{4,12},{6,14},{8,0},{10,2},{12,4},{14,6},{1,9},{3,11}... | collective-permute-start | bytes 6920 | tf_op jit(solution)/shard_map/ppermute | solution.py:292
  21.0 1.9 %collective-permute-start.9 = (f32[3,192]{1,0:T(4,128)S(1)}, f32[3,192]{1,0:T(4,128)S(1)}, u32[]{:S(2)}, u32[]{:S(2)}) collective-permute-start(f32[3,192]{1,0:T(4,128)S(1)} %convert_maximum_fusion), channel_id=1, source_target_pairs={{0,12},{2,14},{4,8},{6,10},{8,4},{10,6},{12,0},{14,2},{1,13},{3,15... | collective-permute-start | bytes 6920 | tf_op jit(solution)/shard_map/ppermute | solution.py:292
  22.9 1.9 %shard_map.84 = bf16[2,2,96,128]{3,2,1,0:T(8,128)(2,1)} custom-call(bf16[4,64,192]{2,1,0:T(8,128)(2,1)S(1)} %get-tuple-element.34.near_merged, bf16[4,64,192]{2,1,0:T(8,128)(2,1)S(1)} %get-tuple-element.37.own_merged, bf16[144,192]{1,0:T(8,128)(2,1)S(1)} %collective-permute-done.6.far_merged, bf16[3,3,96,192]{3,2,1,0:T(8,128)(2,1)S(1)} %copy-done.2), custom_call_target="tpu_custom_call" | custom-call | flops 3000000000 | bytes 1048576 | tf_op jit(solution)/shard_map/pallas_call | solution.py:309
  24.8 1.6 %collective-permute-done.9 = f32[3,192]{1,0:T(4,128)S(1)} collective-permute-done((f32[3,192]{1,0:T(4,128)S(1)}, f32[3,192]{1,0:T(4,128)S(1)}, u32[]{:S(2)}, u32[]{:S(2)}) %collective-permute-start.9) | collective-permute-done | bytes 2336 | tf_op jit(solution)/shard_map/ppermute | solution.py:292
  26.4 0.1 collective-permute-done.7
  26.5 0.6 %maximum_maximum_fusion = f32[3,192]{1,0:T(4,128)} fusion(f32[3,192]{1,0:T(4,128)S(1)} %collective-permute-done.9, f32[3,192]{1,0:T(4,128)S(1)} %collective-permute-done.8, f32[3,192]{1,0:T(4,128)S(1)} %collective-permute-done.7, f32[3,192]{1,0:T(4,128)S(1)} %get-tuple-element.39, bf16[1,192]{1,0:T(2,128)(2,1)S(1)} %slice_maximum_fusion), kind=kLoop, calls=%fused_computation | loop fusion | flops 2880 | bytes 11904 | tf_op jit(solution)/shard_map/max | solution.py:293
  (19 shorter events, 0.1 us)
Async XLA Ops:
  0.6 1.7 %collective-permute-start = (bf16[2,1,64,192]{3,2,1,0:T(8,128)(2,1)}, bf16[2,1,64,192]{3,2,1,0:T(8,128)(2,1)S(1)}, u32[]{:S(2)}, u32[]{:S(2)}) collective-permute-start(bf16[2,1,64,192]{3,2,1,0:T(8,128)(2,1)} %latent.1), channel_id=1, source_target_pairs={{0,1},{1,0},{2,3},{3,2},{4,5},{5,4},{6,7},{7,6},{8,9},{9,8},{10,11... | collective-permute-start | bytes 147464 | tf_op jit(solution)/shard_map/ppermute | solution.py:20
  1.2 0.8 %copy-start.3 = (bf16[2,1,64,192]{3,2,1,0:T(8,128)(2,1)S(1)}, bf16[2,1,64,192]{3,2,1,0:T(8,128)(2,1)}, u32[]{:S(2)}) copy-start(bf16[2,1,64,192]{3,2,1,0:T(8,128)(2,1)} %latent.1) | copy-start | bytes 147460
  2.0 7.3 %copy-start = (bf16[3,3,3,192,192]{4,3,2,1,0:T(8,128)(2,1)S(1)}, bf16[3,3,3,192,192]{4,3,2,1,0:T(8,128)(2,1)}, u32[]{:S(2)}) copy-start(bf16[3,3,3,192,192]{4,3,2,1,0:T(8,128)(2,1)} %weights.7) | copy-start | bytes 5971972
  2.0 7.3 %copy-start.4 = (bf16[192]{0:T(256)(128)(2,1)S(1)}, bf16[192]{0:T(256)(128)(2,1)}, u32[]{:S(2)}) copy-start(bf16[192]{0:T(256)(128)(2,1)} %gain_a.1) | copy-start | bytes 1156
  2.0 7.3 %copy-start.5 = (bf16[192]{0:T(256)(128)(2,1)S(1)}, bf16[192]{0:T(256)(128)(2,1)}, u32[]{:S(2)}) copy-start(bf16[192]{0:T(256)(128)(2,1)} %gain_b.1) | copy-start | bytes 1156
  2.4 9.2 %collective-permute-start.4 = (bf16[6,64,128]{2,1,0:T(8,128)(2,1)S(1)}, bf16[6,64,128]{2,1,0:T(8,128)(2,1)S(1)}, u32[]{:S(2)}, u32[]{:S(2)}) collective-permute-start(bf16[6,64,128]{2,1,0:T(8,128)(2,1)S(1)} %shard_map.78.own), channel_id=1, source_target_pairs={{0,4},{1,0},{2,6},{3,2},{4,8},{5,1},{6,10},{7,3},{8,12},{9,5},{10,... | collective-permute-start | bytes 294920 | tf_op jit(solution)/shard_map/ppermute | solution.py:30
  5.3 8.2 %collective-permute-start.3 = (bf16[6,64,128]{2,1,0:T(8,128)(2,1)S(1)}, bf16[6,64,128]{2,1,0:T(8,128)(2,1)S(1)}, u32[]{:S(2)}, u32[]{:S(2)}) collective-permute-start(bf16[6,64,128]{2,1,0:T(8,128)(2,1)S(1)} %shard_map.78.own), channel_id=1, source_target_pairs={{0,6},{1,0},{2,8},{3,2},{4,10},{5,4},{6,12},{7,1},{8,14},{9,3},{10... | collective-permute-start | bytes 294920 | tf_op jit(solution)/shard_map/ppermute | solution.py:30
  7.8 3.8 %collective-permute-start.1 = (bf16[6,64,128]{2,1,0:T(8,128)(2,1)S(1)}, bf16[6,64,128]{2,1,0:T(8,128)(2,1)S(1)}, u32[]{:S(2)}, u32[]{:S(2)}) collective-permute-start(bf16[6,64,128]{2,1,0:T(8,128)(2,1)S(1)} %shard_map.78.own), channel_id=1, source_target_pairs={{0,2},{1,0},{2,4},{3,1},{4,6},{5,3},{6,8},{7,5},{8,10},{9,7},{10,1... | collective-permute-start | bytes 294920 | tf_op jit(solution)/shard_map/ppermute | solution.py:30
  11.6 2.0 %collective-permute-start.2 = (bf16[6,64,128]{2,1,0:T(8,128)(2,1)S(1)}, bf16[6,64,128]{2,1,0:T(8,128)(2,1)S(1)}, u32[]{:S(2)}, u32[]{:S(2)}) collective-permute-start(bf16[6,64,128]{2,1,0:T(8,128)(2,1)S(1)} %collective-permute-done.1.near_1), channel_id=1, source_target_pairs={{0,1},{1,0},{2,3},{3,2},{4,5},{5,4},{6,7},{7,6},{8,9},{9,8},{10,11... | collective-permute-start | bytes 294920 | tf_op jit(solution)/shard_map/ppermute | solution.py:20
  13.0 1.9 %copy-start.1 = (bf16[3,3,3,192,192]{4,3,2,1,0:T(8,128)(2,1)S(1)}, bf16[3,3,3,192,192]{4,3,2,1,0:T(8,128)(2,1)}, u32[]{:S(2)}) copy-start(bf16[3,3,3,192,192]{4,3,2,1,0:T(8,128)(2,1)} %weights.9) | copy-start | bytes 5971972
  13.0 3.2 %collective-permute-start.5 = (bf16[4,64,256]{2,1,0:T(8,128)(2,1)S(1)}, bf16[4,64,256]{2,1,0:T(8,128)(2,1)S(1)}, u32[]{:S(2)}, u32[]{:S(2)}) collective-permute-start(bf16[4,64,256]{2,1,0:T(8,128)(2,1)S(1)} %get-tuple-element.35), channel_id=1, source_target_pairs={{0,1},{1,0},{2,3},{3,2},{4,5},{5,4},{6,7},{7,6},{8,9},{9,8},{10,11... | collective-permute-start | bytes 393224 | tf_op jit(solution)/shard_map/ppermute | solution.py:20
  15.8 1.3 %collective-permute-start.6 = (bf16[144,192]{1,0:T(8,128)(2,1)S(1)}, bf16[144,192]{1,0:T(8,128)(2,1)S(1)}, u32[]{:S(2)}, u32[]{:S(2)}) collective-permute-start(bf16[144,192]{1,0:T(8,128)(2,1)S(1)} %get-tuple-element.38), channel_id=1, source_target_pairs={{0,1},{1,0},{2,3},{3,2},{4,5},{5,4},{6,7},{7,6},{8,9},{9,8},{10,11... | collective-permute-start | bytes 165896 | tf_op jit(solution)/shard_map/ppermute | solution.py:20
  16.2 6.7 %copy-start.2 = (bf16[3,3,96,192]{3,2,1,0:T(8,128)(2,1)S(1)}, bf16[3,3,96,192]{3,2,1,0:T(8,128)(2,1)}, u32[]{:S(2)}) copy-start(bf16[3,3,96,192]{3,2,1,0:T(8,128)(2,1)} %conv_up.1) | copy-start | bytes 995332
  17.1 7.7 %collective-permute-start.8 = (f32[3,192]{1,0:T(4,128)S(1)}, f32[3,192]{1,0:T(4,128)S(1)}, u32[]{:S(2)}, u32[]{:S(2)}) collective-permute-start(f32[3,192]{1,0:T(4,128)S(1)} %convert_maximum_fusion), channel_id=1, source_target_pairs={{0,8},{2,10},{4,12},{6,14},{8,0},{10,2},{12,4},{14,6},{1,9},{3,11}... | collective-permute-start | bytes 6920 | tf_op jit(solution)/shard_map/ppermute | solution.py:292
  21.0 5.4 %collective-permute-start.9 = (f32[3,192]{1,0:T(4,128)S(1)}, f32[3,192]{1,0:T(4,128)S(1)}, u32[]{:S(2)}, u32[]{:S(2)}) collective-permute-start(f32[3,192]{1,0:T(4,128)S(1)} %convert_maximum_fusion), channel_id=1, source_target_pairs={{0,12},{2,14},{4,8},{6,10},{8,4},{10,6},{12,0},{14,2},{1,13},{3,15... | collective-permute-start | bytes 6920 | tf_op jit(solution)/shard_map/ppermute | solution.py:292
  22.9 3.6 %collective-permute-start.7 = (f32[3,192]{1,0:T(4,128)S(1)}, f32[3,192]{1,0:T(4,128)S(1)}, u32[]{:S(2)}, u32[]{:S(2)}) collective-permute-start(f32[3,192]{1,0:T(4,128)S(1)} %convert_maximum_fusion), channel_id=1, source_target_pairs={{0,4},{2,6},{4,0},{6,2},{8,12},{10,14},{12,8},{14,10},{1,5},{3,7},... | collective-permute-start | bytes 6920 | tf_op jit(solution)/shard_map/ppermute | solution.py:292

commit v2 on v1

--- a/solution.py
+++ b/solution.py
@@ -284,13 +284,23 @@
     return rounds
 
 
+def flipped(peaks, flip_0, flip_1):
+    route = []
+    for row in range(lax.axis_size("rows")):
+        route.append((2 * row, 2 * (row ^ flip_0)))
+        route.append((2 * row + 1, 2 * (row ^ flip_1) + 1))
+    return lax.ppermute(peaks, ("rows", "tm"), route)
+
+
 def group_peaks(peaks):
-    rows = lax.axis_size("rows")
-    for flips in peak_rounds(rows):
-        arrived = []
-        for flip in flips:
-            arrived.append(lax.ppermute(peaks, "rows", [(r, r ^ flip) for r in range(rows)]))
-        peaks = functools.reduce(jnp.maximum, arrived, peaks)
+    for flips in peak_rounds(lax.axis_size("rows")):
+        turns = [(flips[0], flips[2]), (flips[1], flips[0])] if len(flips) == 3 else [flips * 2]
+        arrived = [peaks]
+        for flip_0, flip_1 in turns:
+            arrived.append(flipped(peaks, flip_0, flip_1))
+        peaks = functools.reduce(jnp.maximum, arrived)
+        if len(flips) == 3:
+            peaks = jnp.maximum(peaks, swap_cores(peaks))
     return peaks
 
 

time: 27.3 us -> 27.6 us (1.011)
  waiting for transfers between devices: 3.36 us -> 5.07 us
  starting transfers between devices: 14.3 us -> 12.8 us
    ppermute x3 -> x2, starting transfers between devices: 5.77 us -> 4.04 us  [flipped(): return lax.ppermute(peaks, ('rows', 'tm'), route)]
    ppermute x3 -> x2, waiting for transfers between devices: 1.72 us -> 3.43 us  [flipped(): return lax.ppermute(peaks, ('rows', 'tm'), route)]
    ppermute x4 -> x5, starting transfers between devices: 1.54 us -> 1.83 us  [swap_cores(): return lax.ppermute(block, 'tm', [(0, 1), (1, 0)])]
    max x1 -> x2, other arithmetic: 0.6 us -> 0.61 us  [the longest x1 0.6 us: group_peaks(): peaks = jnp.maximum(peaks, swap_cores(peaks))]
  transfers between devices with their start and end apart: 10 -> 10, of which waited for: 4 -> 4; matrix products, arithmetic and copies ran while one was open for 0% -> 0% of each run, Pallas kernels for 27% -> 26%
where the time goes in v2:
time: 27.6 us; the launch traced here: 27.4 us
  starting transfers between devices  12.8 us (46%)
  Pallas kernels  7.29 us (26%)
  waiting for transfers between devices  5.07 us (18%)
  local copies, waits for them, and re-layouts  0.87 us (3%)
  between operations  0.73 us (3%)
  other arithmetic  0.62 us (2%)
    pallas_call x8, Pallas kernels, call(): pl.pallas_call(kernel, out_shape=outs, in_specs=[VMEM] * len(operands), o...  7.29 us
    ppermute x3, starting transfers between devices, near_rows(): return lax.ppermute(block, ('rows', 'tm'), route)  6.96 us
    ppermute x2, starting transfers between devices, flipped(): return lax.ppermute(peaks, ('rows', 'tm'), route)  4.04 us
    ppermute x2, waiting for transfers between devices, flipped(): return lax.ppermute(peaks, ('rows', 'tm'), route)  3.43 us
    ppermute x5, starting transfers between devices, swap_cores(): return lax.ppermute(block, 'tm', [(0, 1), (1, 0)])  1.83 us
    ppermute x3, waiting for transfers between devices, near_rows(): return lax.ppermute(block, ('rows', 'tm'), route)  1.39 us
    unnamed x12, local copies, waits for them, and re-layouts  0.87 us
    max x1, other arithmetic, group_peaks(): peaks = jnp.maximum(peaks, swap_cores(peaks))  0.6 us
  transfers between devices with their start and end apart: 10, of which 4 were waited for; matrix products, arithmetic and copies ran while one was open for 0% of the time, Pallas kernels for 26%

profile of v2, /device:TPU:0, one launch (start us, length us, event | category | flops | bytes accessed | tf_op | source)
XLA Modules:
  0.0 27.4 jit_solution(6739752131844922333)
XLA Ops:
  0.6 0.6 %collective-permute-start = (bf16[2,1,64,192]{3,2,1,0:T(8,128)(2,1)}, bf16[2,1,64,192]{3,2,1,0:T(8,128)(2,1)S(1)}, u32[]{:S(2)}, u32[]{:S(2)}) collective-permute-start(bf16[2,1,64,192]{3,2,1,0:T(8,128)(2,1)} %latent.1), channel_id=1, source_target_pairs={{0,1},{1,0},{2,3},{3,2},{4,5},{5,4},{6,7},{7,6},{8,9},{9,8},{10,11... | collective-permute-start | bytes 147464 | tf_op jit(solution)/shard_map/ppermute | solution.py:20
  1.2 0.8 %copy-done.3 = bf16[2,1,64,192]{3,2,1,0:T(8,128)(2,1)S(1)} copy-done((bf16[2,1,64,192]{3,2,1,0:T(8,128)(2,1)S(1)}, bf16[2,1,64,192]{3,2,1,0:T(8,128)(2,1)}, u32[]{:S(2)}) %copy-start.3) | copy-done | bytes 49176
  2.0 0.0 copy-start.5
  2.1 0.2 collective-permute-done.other
  2.3 0.1 shard_map.78.own
  2.4 2.9 %collective-permute-start.4 = (bf16[6,64,128]{2,1,0:T(8,128)(2,1)S(1)}, bf16[6,64,128]{2,1,0:T(8,128)(2,1)S(1)}, u32[]{:S(2)}, u32[]{:S(2)}) collective-permute-start(bf16[6,64,128]{2,1,0:T(8,128)(2,1)S(1)} %shard_map.78.own), channel_id=1, source_target_pairs={{0,4},{1,0},{2,6},{3,2},{4,8},{5,1},{6,10},{7,3},{8,12},{9,5},{10,... | collective-permute-start | bytes 294920 | tf_op jit(solution)/shard_map/ppermute | solution.py:30
  5.3 2.5 %collective-permute-start.3 = (bf16[6,64,128]{2,1,0:T(8,128)(2,1)S(1)}, bf16[6,64,128]{2,1,0:T(8,128)(2,1)S(1)}, u32[]{:S(2)}, u32[]{:S(2)}) collective-permute-start(bf16[6,64,128]{2,1,0:T(8,128)(2,1)S(1)} %shard_map.78.own), channel_id=1, source_target_pairs={{0,6},{1,0},{2,8},{3,2},{4,10},{5,4},{6,12},{7,1},{8,14},{9,3},{10... | collective-permute-start | bytes 294920 | tf_op jit(solution)/shard_map/ppermute | solution.py:30
  7.8 1.5 %collective-permute-start.1 = (bf16[6,64,128]{2,1,0:T(8,128)(2,1)S(1)}, bf16[6,64,128]{2,1,0:T(8,128)(2,1)S(1)}, u32[]{:S(2)}, u32[]{:S(2)}) collective-permute-start(bf16[6,64,128]{2,1,0:T(8,128)(2,1)S(1)} %shard_map.78.own), channel_id=1, source_target_pairs={{0,2},{1,0},{2,4},{3,1},{4,6},{5,3},{6,8},{7,5},{8,10},{9,7},{10,1... | collective-permute-start | bytes 294920 | tf_op jit(solution)/shard_map/ppermute | solution.py:30
  9.4 0.8 %shard_map.79 = (f32[1,4,64,192]{3,2,1,0:T(8,128)S(1)}, f32[1,4,64,192]{3,2,1,0:T(8,128)S(1)}, f32[1,256]{1,0:T(1,128)S(1)}, f32[1,256]{1,0:T(1,128)S(1)}, f32[1,256]{1,0:T(1,128)S(1)}) custom-call(bf16[6,64,128]{2,1,0:T(8,128)(2,1)S(1)} %shard_map.78.own, bf16[192]{0:T(256)(128)(2,1)S(1)} %copy-done.4, bf16[192]{0:T(256)(128)(2,1)S(1)} %copy-done.5, ...), custom_call_target="tpu_custom_call" | custom-call | flops 3000000000 | bytes 1048576 | tf_op jit(solution)/shard_map/pallas_call | solution.py:319
  10.2 1.4 %collective-permute-done.1.near_1 = bf16[6,64,128]{2,1,0:T(8,128)(2,1)S(1)} collective-permute-done((bf16[6,64,128]{2,1,0:T(8,128)(2,1)S(1)}, bf16[6,64,128]{2,1,0:T(8,128)(2,1)S(1)}, u32[]{:S(2)}, u32[]{:S(2)}) %collective-permute-start.1) | collective-permute-done | bytes 98336 | tf_op jit(solution)/shard_map/ppermute | solution.py:30
  11.6 1.4 %shard_map.80 = (bf16[1,4,3,64,256]{4,3,2,1,0:T(8,128)(2,1)S(1)}, bf16[1,4,3,64,256]{4,3,2,1,0:T(8,128)(2,1)S(1)}, bf16[4,64,256]{2,1,0:T(8,128)(2,1)S(1)}, f32[1,4,64,192]{3,2,1,0:T(8,128)S(1)}, f32[2,256]{1,0:T(2,128)S(1)}) custom-call(bf16[6,64,128]{2,1,0:T(8,128)(2,1)S(1)} %collective-permute-done.1.near_1, ...), custom_call_target="tpu_custom_call" | custom-call | flops 3000000000 | bytes 1048576 | tf_op jit(solution)/shard_map/pallas_call | solution.py:319
  13.0 0.0 copy-start.1
  13.0 0.6 %collective-permute-start.5 = (bf16[4,64,256]{2,1,0:T(8,128)(2,1)S(1)}, bf16[4,64,256]{2,1,0:T(8,128)(2,1)S(1)}, u32[]{:S(2)}, u32[]{:S(2)}) collective-permute-start(bf16[4,64,256]{2,1,0:T(8,128)(2,1)S(1)} %get-tuple-element.35), channel_id=1, source_target_pairs={{0,1},{1,0},{2,3},{3,2},{4,5},{5,4},{6,7},{7,6},{8,9},{9,8},{10,11... | collective-permute-start | bytes 393224 | tf_op jit(solution)/shard_map/ppermute | solution.py:20
  13.5 1.3 %shard_map.81 = (bf16[1,4,3,64,256]{4,3,2,1,0:T(8,128)(2,1)S(1)}, bf16[1,4,3,64,256]{4,3,2,1,0:T(8,128)(2,1)S(1)}, f32[2,256]{1,0:T(2,128)S(1)}) custom-call(bf16[6,64,128]{2,1,0:T(8,128)(2,1)S(1)} %collective-permute-done.2.far_1, bf16[6,64,128]{2,1,0:T(8,128)(2,1)S(1)} %collective-permute-done.3.near_3, ...), custom_call_target="tpu_custom_call" | custom-call | flops 750000000 | bytes 1048576 | tf_op jit(solution)/shard_map/pallas_call | solution.py:319
  14.8 0.9 %shard_map.82 = (bf16[4,64,192]{2,1,0:T(8,128)(2,1)S(1)}, bf16[144,192]{1,0:T(8,128)(2,1)S(1)}) custom-call(bf16[6,64,128]{2,1,0:T(8,128)(2,1)S(1)} %collective-permute-done.1.near_1, bf16[1,4,3,64,256]{4,3,2,1,0:T(8,128)(2,1)S(1)} %get-tuple-element.31.taps_2, bf16[1,4,3,64,256]{4,3,2,1,0:T(8,128)(2,1)S(1)} %get-tuple-element.32.taps_1, ...), custom_call_target="tpu_custom_call" | custom-call | flops 3000000000 | bytes 1048576 | tf_op jit(solution)/shard_map/pallas_call | solution.py:319
  15.8 0.4 %collective-permute-start.6 = (bf16[144,192]{1,0:T(8,128)(2,1)S(1)}, bf16[144,192]{1,0:T(8,128)(2,1)S(1)}, u32[]{:S(2)}, u32[]{:S(2)}) collective-permute-start(bf16[144,192]{1,0:T(8,128)(2,1)S(1)} %get-tuple-element.38), channel_id=1, source_target_pairs={{0,1},{1,0},{2,3},{3,2},{4,5},{5,4},{6,7},{7,6},{8,9},{9,8},{10,11... | collective-permute-start | bytes 165896 | tf_op jit(solution)/shard_map/ppermute | solution.py:20
  16.2 0.9 %shard_map.83 = (bf16[4,64,192]{2,1,0:T(8,128)(2,1)S(1)}, f32[3,192]{1,0:T(4,128)S(1)}) custom-call(bf16[6,64,128]{2,1,0:T(8,128)(2,1)S(1)} %shard_map.78.own, bf16[1,4,3,64,256]{4,3,2,1,0:T(8,128)(2,1)S(1)} %get-tuple-element.32.taps_1, bf16[1,4,3,64,256]{4,3,2,1,0:T(8,128)(2,1)S(1)} %get-tuple-element.33.taps_0, ...), custom_call_target="tpu_custom_call" | custom-call | flops 3000000000 | bytes 1048576 | tf_op jit(solution)/shard_map/pallas_call | solution.py:319
  17.1 3.9 %collective-permute-start.8 = (f32[3,192]{1,0:T(4,128)S(1)}, f32[3,192]{1,0:T(4,128)S(1)}, u32[]{:S(2)}, u32[]{:S(2)}) collective-permute-start(f32[3,192]{1,0:T(4,128)S(1)} %convert_maximum_fusion), channel_id=1, source_target_pairs={{0,8},{1,5},{2,10},{3,7},{4,12},{5,1},{6,14},{7,3},{8,0},{9,13},{1... | collective-permute-start | bytes 6920 | tf_op jit(solution)/shard_map/ppermute | solution.py:292
  21.0 0.2 collective-permute-start.7
  21.2 1.4 %collective-permute-done.8 = f32[3,192]{1,0:T(4,128)S(1)} collective-permute-done((f32[3,192]{1,0:T(4,128)S(1)}, f32[3,192]{1,0:T(4,128)S(1)}, u32[]{:S(2)}, u32[]{:S(2)}) %collective-permute-start.8) | collective-permute-done | bytes 2336 | tf_op jit(solution)/shard_map/ppermute | solution.py:292
  22.6 2.0 %collective-permute-done.7 = f32[3,192]{1,0:T(4,128)S(1)} collective-permute-done((f32[3,192]{1,0:T(4,128)S(1)}, f32[3,192]{1,0:T(4,128)S(1)}, u32[]{:S(2)}, u32[]{:S(2)}) %collective-permute-start.7) | collective-permute-done | bytes 2336 | tf_op jit(solution)/shard_map/ppermute | solution.py:292
  24.6 0.3 %collective-permute-start.9 = (f32[3,192]{1,0:T(4,128)S(1)}, f32[3,192]{1,0:T(4,128)S(1)}, u32[]{:S(2)}, u32[]{:S(2)}) collective-permute-start(f32[3,192]{1,0:T(4,128)S(1)} %maximum_maximum_fusion), channel_id=1, source_target_pairs={{0,1},{1,0},{2,3},{3,2},{4,5},{5,4},{6,7},{7,6},{8,9},{9,8},{10,11... | collective-permute-start | bytes 6920 | tf_op jit(solution)/shard_map/ppermute | solution.py:20
  24.9 1.9 %shard_map.84 = bf16[2,2,96,128]{3,2,1,0:T(8,128)(2,1)} custom-call(bf16[4,64,192]{2,1,0:T(8,128)(2,1)S(1)} %get-tuple-element.34.near_merged, bf16[4,64,192]{2,1,0:T(8,128)(2,1)S(1)} %get-tuple-element.37.own_merged, bf16[144,192]{1,0:T(8,128)(2,1)S(1)} %collective-permute-done.6.far_merged, bf16[3,3,96,192]{3,2,1,0:T(8,128)(2,1)S(1)} %copy-done.2), custom_call_target="tpu_custom_call" | custom-call | flops 3000000000 | bytes 1048576 | tf_op jit(solution)/shard_map/pallas_call | solution.py:319
  26.8 0.6 %max.20 = f32[3,192]{1,0:T(4,128)} maximum(f32[3,192]{1,0:T(4,128)S(1)} %maximum_maximum_fusion, f32[3,192]{1,0:T(4,128)S(1)} %collective-permute-done.9) | non-fusion elementwise | flops 576 | bytes 6912 | tf_op jit(solution)/shard_map/max | solution.py:303
  (20 shorter events, 0.1 us)
Async XLA Ops:
  0.6 1.7 %collective-permute-start = (bf16[2,1,64,192]{3,2,1,0:T(8,128)(2,1)}, bf16[2,1,64,192]{3,2,1,0:T(8,128)(2,1)S(1)}, u32[]{:S(2)}, u32[]{:S(2)}) collective-permute-start(bf16[2,1,64,192]{3,2,1,0:T(8,128)(2,1)} %latent.1), channel_id=1, source_target_pairs={{0,1},{1,0},{2,3},{3,2},{4,5},{5,4},{6,7},{7,6},{8,9},{9,8},{10,11... | collective-permute-start | bytes 147464 | tf_op jit(solution)/shard_map/ppermute | solution.py:20
  1.2 0.8 %copy-start.3 = (bf16[2,1,64,192]{3,2,1,0:T(8,128)(2,1)S(1)}, bf16[2,1,64,192]{3,2,1,0:T(8,128)(2,1)}, u32[]{:S(2)}) copy-start(bf16[2,1,64,192]{3,2,1,0:T(8,128)(2,1)} %latent.1) | copy-start | bytes 147460
  2.0 7.3 %copy-start = (bf16[3,3,3,192,192]{4,3,2,1,0:T(8,128)(2,1)S(1)}, bf16[3,3,3,192,192]{4,3,2,1,0:T(8,128)(2,1)}, u32[]{:S(2)}) copy-start(bf16[3,3,3,192,192]{4,3,2,1,0:T(8,128)(2,1)} %weights.7) | copy-start | bytes 5971972
  2.0 7.3 %copy-start.4 = (bf16[192]{0:T(256)(128)(2,1)S(1)}, bf16[192]{0:T(256)(128)(2,1)}, u32[]{:S(2)}) copy-start(bf16[192]{0:T(256)(128)(2,1)} %gain_a.1) | copy-start | bytes 1156
  2.0 7.3 %copy-start.5 = (bf16[192]{0:T(256)(128)(2,1)S(1)}, bf16[192]{0:T(256)(128)(2,1)}, u32[]{:S(2)}) copy-start(bf16[192]{0:T(256)(128)(2,1)} %gain_b.1) | copy-start | bytes 1156
  2.4 9.2 %collective-permute-start.4 = (bf16[6,64,128]{2,1,0:T(8,128)(2,1)S(1)}, bf16[6,64,128]{2,1,0:T(8,128)(2,1)S(1)}, u32[]{:S(2)}, u32[]{:S(2)}) collective-permute-start(bf16[6,64,128]{2,1,0:T(8,128)(2,1)S(1)} %shard_map.78.own), channel_id=1, source_target_pairs={{0,4},{1,0},{2,6},{3,2},{4,8},{5,1},{6,10},{7,3},{8,12},{9,5},{10,... | collective-permute-start | bytes 294920 | tf_op jit(solution)/shard_map/ppermute | solution.py:30
  5.3 8.2 %collective-permute-start.3 = (bf16[6,64,128]{2,1,0:T(8,128)(2,1)S(1)}, bf16[6,64,128]{2,1,0:T(8,128)(2,1)S(1)}, u32[]{:S(2)}, u32[]{:S(2)}) collective-permute-start(bf16[6,64,128]{2,1,0:T(8,128)(2,1)S(1)} %shard_map.78.own), channel_id=1, source_target_pairs={{0,6},{1,0},{2,8},{3,2},{4,10},{5,4},{6,12},{7,1},{8,14},{9,3},{10... | collective-permute-start | bytes 294920 | tf_op jit(solution)/shard_map/ppermute | solution.py:30
  7.8 3.8 %collective-permute-start.1 = (bf16[6,64,128]{2,1,0:T(8,128)(2,1)S(1)}, bf16[6,64,128]{2,1,0:T(8,128)(2,1)S(1)}, u32[]{:S(2)}, u32[]{:S(2)}) collective-permute-start(bf16[6,64,128]{2,1,0:T(8,128)(2,1)S(1)} %shard_map.78.own), channel_id=1, source_target_pairs={{0,2},{1,0},{2,4},{3,1},{4,6},{5,3},{6,8},{7,5},{8,10},{9,7},{10,1... | collective-permute-start | bytes 294920 | tf_op jit(solution)/shard_map/ppermute | solution.py:30
  11.6 2.0 %collective-permute-start.2 = (bf16[6,64,128]{2,1,0:T(8,128)(2,1)S(1)}, bf16[6,64,128]{2,1,0:T(8,128)(2,1)S(1)}, u32[]{:S(2)}, u32[]{:S(2)}) collective-permute-start(bf16[6,64,128]{2,1,0:T(8,128)(2,1)S(1)} %collective-permute-done.1.near_1), channel_id=1, source_target_pairs={{0,1},{1,0},{2,3},{3,2},{4,5},{5,4},{6,7},{7,6},{8,9},{9,8},{10,11... | collective-permute-start | bytes 294920 | tf_op jit(solution)/shard_map/ppermute | solution.py:20
  13.0 1.9 %copy-start.1 = (bf16[3,3,3,192,192]{4,3,2,1,0:T(8,128)(2,1)S(1)}, bf16[3,3,3,192,192]{4,3,2,1,0:T(8,128)(2,1)}, u32[]{:S(2)}) copy-start(bf16[3,3,3,192,192]{4,3,2,1,0:T(8,128)(2,1)} %weights.9) | copy-start | bytes 5971972
  13.0 3.2 %collective-permute-start.5 = (bf16[4,64,256]{2,1,0:T(8,128)(2,1)S(1)}, bf16[4,64,256]{2,1,0:T(8,128)(2,1)S(1)}, u32[]{:S(2)}, u32[]{:S(2)}) collective-permute-start(bf16[4,64,256]{2,1,0:T(8,128)(2,1)S(1)} %get-tuple-element.35), channel_id=1, source_target_pairs={{0,1},{1,0},{2,3},{3,2},{4,5},{5,4},{6,7},{7,6},{8,9},{9,8},{10,11... | collective-permute-start | bytes 393224 | tf_op jit(solution)/shard_map/ppermute | solution.py:20
  15.8 1.3 %collective-permute-start.6 = (bf16[144,192]{1,0:T(8,128)(2,1)S(1)}, bf16[144,192]{1,0:T(8,128)(2,1)S(1)}, u32[]{:S(2)}, u32[]{:S(2)}) collective-permute-start(bf16[144,192]{1,0:T(8,128)(2,1)S(1)} %get-tuple-element.38), channel_id=1, source_target_pairs={{0,1},{1,0},{2,3},{3,2},{4,5},{5,4},{6,7},{7,6},{8,9},{9,8},{10,11... | collective-permute-start | bytes 165896 | tf_op jit(solution)/shard_map/ppermute | solution.py:20
  16.2 8.7 %copy-start.2 = (bf16[3,3,96,192]{3,2,1,0:T(8,128)(2,1)S(1)}, bf16[3,3,96,192]{3,2,1,0:T(8,128)(2,1)}, u32[]{:S(2)}) copy-start(bf16[3,3,96,192]{3,2,1,0:T(8,128)(2,1)} %conv_up.1) | copy-start | bytes 995332
  17.1 5.5 %collective-permute-start.8 = (f32[3,192]{1,0:T(4,128)S(1)}, f32[3,192]{1,0:T(4,128)S(1)}, u32[]{:S(2)}, u32[]{:S(2)}) collective-permute-start(f32[3,192]{1,0:T(4,128)S(1)} %convert_maximum_fusion), channel_id=1, source_target_pairs={{0,8},{1,5},{2,10},{3,7},{4,12},{5,1},{6,14},{7,3},{8,0},{9,13},{1... | collective-permute-start | bytes 6920 | tf_op jit(solution)/shard_map/ppermute | solution.py:292
  21.0 3.6 %collective-permute-start.7 = (f32[3,192]{1,0:T(4,128)S(1)}, f32[3,192]{1,0:T(4,128)S(1)}, u32[]{:S(2)}, u32[]{:S(2)}) collective-permute-start(f32[3,192]{1,0:T(4,128)S(1)} %convert_maximum_fusion), channel_id=1, source_target_pairs={{0,4},{1,13},{2,6},{3,15},{4,0},{5,9},{6,2},{7,11},{8,12},{9,5},{1... | collective-permute-start | bytes 6920 | tf_op jit(solution)/shard_map/ppermute | solution.py:292
  24.6 2.2 %collective-permute-start.9 = (f32[3,192]{1,0:T(4,128)S(1)}, f32[3,192]{1,0:T(4,128)S(1)}, u32[]{:S(2)}, u32[]{:S(2)}) collective-permute-start(f32[3,192]{1,0:T(4,128)S(1)} %maximum_maximum_fusion), channel_id=1, source_target_pairs={{0,1},{1,0},{2,3},{3,2},{4,5},{5,4},{6,7},{7,6},{8,9},{9,8},{10,11... | collective-permute-start | bytes 6920 | tf_op jit(solution)/shard_map/ppermute | solution.py:20
